TPU v7x, 256 devices: a whole 4x4x8 slice. The times are simulated.
256 devices in a mesh: inst: 16 (over x, y), page: 8 (over z), head: 2 (over core).
Axes of the slice: x: 4, y: 4, z: 8, core: 2. Of those that a mesh axis runs over, the one named last changes fastest.
Arguments:
- queries: bfloat16 [32, 8192], P('inst', 'head'), may hold values from -21 to 21
- fresh_key_value: bfloat16 [2, 32, 1024], P(None, 'inst', 'head'), may hold values from -8 to 8
- key_value_pool: bfloat16 [2, 16384, 16, 1024], P(None, ('inst', 'page'), None, 'head'), may hold values from -21 to 21
- block_table: int32 [32, 768], P('inst'), may hold values from -1 to 16383, as said below
- lengths: int32 [32], P('inst'), may hold values from 17 to 12288, as said below
Outputs:
- attn: bfloat16 [32, 8192], P('inst', 'head')
Inputs may be any that keep to these rules, and one draw needn't show every extreme that they name: `block_table`: request r is owned by instance r // 2. Entries 0 to ceil(lengths[r] / 16) - 1 of row r are pool page numbers below 16384, distinct over all requests; every other entry is -1. `lengths`: every request has two or more pages; some request has exactly 768 full pages.
All inputs are finite; a program needn't handle non-finite values.
Results may differ from a plain program's by a relative error of at most 0.001.
Values may be sent and summed in bfloat16 or wider, within the bound.
No kernel may reach another device: no remote copies, remote signals or barrier semaphores. Data moves between devices by JAX's collectives and lax.ppermute only.
A program may use at most 192 MiB of HBM per device.

v0:
```python
import math
import jax
import jax.numpy as jnp
from jax import lax
from jax.sharding import PartitionSpec as P

HEAD_SIZE = 128
LOWEST_SCORE = -1e30


def slot_owners(all_tables, all_lengths, slots, page_tok):
    requests, most_pages = all_tables.shape
    first_page = (lax.axis_index("inst") * lax.axis_size("page") + lax.axis_index("page")) * slots
    column = jnp.arange(most_pages, dtype=jnp.int32)
    live_page = column[None, :] * page_tok < all_lengths[:, None]
    local_page = all_tables - first_page
    inside = live_page & (local_page >= 0) & (local_page < slots)
    expected_output = jnp.where(inside, local_page, slots).reshape(-1)
    request_ids = jnp.broadcast_to(
        jnp.arange(requests, dtype=jnp.int32)[:, None], (requests, most_pages)
    ).reshape(-1)
    page_fill = jnp.clip(all_lengths[:, None] - column[None, :] * page_tok, 0, page_tok).reshape(-1)
    page_owner = (
        jnp.full((slots,), requests, jnp.int32).at[expected_output].set(request_ids, mode="drop")
    )
    filled = jnp.zeros((slots,), jnp.int32).at[expected_output].set(page_fill, mode="drop")
    return (page_owner, filled)


def page_partials(slot_queries, key_value_pool, filled):
    slots = key_value_pool.shape[1]
    page_tok = key_value_pool.shape[2]
    groups = key_value_pool.shape[3] // HEAD_SIZE
    heads = slot_queries.shape[1] // HEAD_SIZE
    grouped_queries = slot_queries.reshape(slots, groups, heads // groups, HEAD_SIZE)
    paged_keys = key_value_pool[0].reshape(slots, page_tok, groups, HEAD_SIZE)
    paged_values = key_value_pool[1].reshape(slots, page_tok, groups, HEAD_SIZE)
    scores = jnp.einsum(
        "sgqd,stgd->sgqt", grouped_queries, paged_keys, preferred_element_type=jnp.float32
    ) * (1.0 / math.sqrt(HEAD_SIZE))
    offsets = jnp.arange(page_tok, dtype=jnp.int32)
    valid = (offsets[None, :] < filled[:, None])[:, None, None, :]
    masked = jnp.where(valid, scores, LOWEST_SCORE)
    page_max = jnp.max(masked, axis=3)
    raw_weight = jnp.where(valid, jnp.exp(masked - page_max[..., None]), 0.0)
    page_sum = jnp.sum(raw_weight, axis=3)
    page_out = jnp.einsum(
        "sgqt,stgd->sgqd",
        raw_weight.astype(jnp.bfloat16),
        paged_values,
        preferred_element_type=jnp.float32,
    )
    return (
        page_max.reshape(slots, heads),
        page_sum.reshape(slots, heads),
        page_out.reshape(slots, heads * HEAD_SIZE),
    )


def request_max(page_max, page_owner, requests):
    matches = page_owner[None, :] == jnp.arange(requests, dtype=jnp.int32)[:, None]
    return jnp.max(jnp.where(matches[:, :, None], page_max[None], LOWEST_SCORE), axis=1)


def request_sums(page_max, page_sum, page_out, page_owner, shared_max):
    requests, heads = shared_max.shape
    slots = page_max.shape[0]
    padded = jnp.concatenate([shared_max, jnp.full((1, heads), LOWEST_SCORE, jnp.float32)], axis=0)
    factor = jnp.exp(page_max - padded[page_owner])
    one_hot = (page_owner[None, :] == jnp.arange(requests, dtype=jnp.int32)[:, None]).astype(
        jnp.float32
    )
    scaled_out = (page_out.reshape(slots, heads, HEAD_SIZE) * factor[:, :, None]).reshape(
        slots, heads * HEAD_SIZE
    )
    summed_out = jnp.dot(
        one_hot, scaled_out, precision=lax.Precision.HIGHEST, preferred_element_type=jnp.float32
    )
    summed_total = jnp.dot(
        one_hot,
        page_sum * factor,
        precision=lax.Precision.HIGHEST,
        preferred_element_type=jnp.float32,
    )
    return (summed_total, summed_out)


def finish(queries, fresh_key_value, cache_max, cache_total, cache_out):
    own_rows = queries.shape[0]
    heads = queries.shape[1] // HEAD_SIZE
    groups = fresh_key_value.shape[2] // HEAD_SIZE
    per_group = heads // groups
    grouped_queries = queries.reshape(own_rows, groups, per_group, HEAD_SIZE)
    new_keys = fresh_key_value[0].reshape(own_rows, groups, HEAD_SIZE)
    fresh_score = jnp.einsum(
        "rgqd,rgd->rgq", grouped_queries, new_keys, preferred_element_type=jnp.float32
    ).reshape(own_rows, heads) * (1.0 / math.sqrt(HEAD_SIZE))
    top_score = jnp.maximum(cache_max, fresh_score)
    carried = jnp.exp(cache_max - top_score)
    own_weight = jnp.exp(fresh_score - top_score)
    denominator = own_weight + cache_total * carried
    new_values = jnp.broadcast_to(
        fresh_key_value[1].astype(jnp.float32).reshape(own_rows, groups, 1, HEAD_SIZE),
        (own_rows, groups, per_group, HEAD_SIZE),
    ).reshape(own_rows, heads, HEAD_SIZE)
    weighted = (
        own_weight[:, :, None] * new_values
        + cache_out.reshape(own_rows, heads, HEAD_SIZE) * carried[:, :, None]
    )
    return (
        (weighted / denominator[:, :, None])
        .reshape(own_rows, heads * HEAD_SIZE)
        .astype(jnp.bfloat16)
    )


def shards(queries, fresh_key_value, key_value_pool, block_table, lengths):
    all_tables, all_lengths = (
        lax.all_gather(block_table, "inst", axis=0, tiled=True),
        lax.all_gather(lengths, "inst", axis=0, tiled=True),
    )
    all_queries = lax.all_gather(queries, "inst", axis=0, tiled=True)
    requests = all_tables.shape[0]
    own_rows = queries.shape[0]
    row_start = lax.axis_index("inst") * own_rows
    page_owner, filled = slot_owners(
        all_tables, all_lengths, key_value_pool.shape[1], key_value_pool.shape[2]
    )
    slot_queries = all_queries[jnp.minimum(page_owner, requests - 1)]
    page_max, page_sum, page_out = page_partials(slot_queries, key_value_pool, filled)
    local_max = request_max(page_max, page_owner, requests)
    shared_max = lax.pmax(local_max, ("inst", "page"))
    shared_total, shared_out = request_sums(page_max, page_sum, page_out, page_owner, shared_max)
    summed_out, summed_total = lax.psum((shared_out, shared_total), ("inst", "page"))
    cache_max = lax.dynamic_slice_in_dim(shared_max, row_start, own_rows, 0)
    cache_total = lax.dynamic_slice_in_dim(summed_total, row_start, own_rows, 0)
    cache_out = lax.dynamic_slice_in_dim(summed_out, row_start, own_rows, 0)
    return finish(queries, fresh_key_value, cache_max, cache_total, cache_out)


def solution(mesh):
    return jax.shard_map(
        shards,
        mesh=mesh,
        in_specs=(
            P("inst", "head"),
            P(None, "inst", "head"),
            P(None, ("inst", "page"), None, "head"),
            P("inst", None),
            P("inst"),
        ),
        out_specs=P("inst", "head"),
        check_vma=False,
    )
```

profile of v0, /device:TPU:0, one launch (start us, length us, event | category | flops | bytes accessed | tf_op | source)
XLA Modules:
  0.0 1664.2 jit_solution(2714726597789726109)
XLA Ops:
  6.5 0.0 all-reduce.4.cloned.1.call-start
  6.5 1.3 dynamic-slice
  8.5 0.9 dynamic-update-slice
  9.3 14.7 all-reduce.1
  24.0 21.6 %all-gather = s32[16,2,768]{2,1,0:T(2,128)S(1)} all-gather(s32[1,2,768]{2,1,0:T(2,128)} %bitcast.89), channel_id=1, replica_groups=mesh['inst'=16,'page'=8,'head'=2] {'inst'}, dimensions={0}, use_global_device_ids=true | all-gather | bytes 104448 | tf_op jit(solution)/shard_map/all_gather | solution.py:119
  45.7 0.1 reshape.177
  45.8 0.1 subtract_clamp_fusion
  45.9 0.1 copy.36
  46.0 0.1 compare_select_fusion
  46.1 90.2 %scatter_custom_fusion = s32[128]{0:T(128)S(1)} fusion(s32[24576]{0:T(1024)S(1)} %bitcast.84, s32[24576]{0:T(1024)S(1)} %reshape.155, s32[]{:T(128)} %constant.17.clone.1), kind=kCustom, calls=%fused_computation.59 | custom fusion | bytes 516 | tf_op jit(solution)/shard_map/scatter | solution.py:24
  136.3 90.2 %scatter_custom_fusion.1 = s32[128]{0:T(128)S(1)} fusion(s32[24576]{0:T(1024)S(1)} %bitcast.85, s32[24576]{0:T(1024)S(1)} %reshape.163, s32[]{:T(128)} %constant.5.clone.1), kind=kCustom, calls=%fused_computation.57 | custom fusion | bytes 516 | tf_op jit(solution)/shard_map/scatter | solution.py:26
  226.5 0.1 iota_compare_fusion
  226.6 22.9 %all-gather.1 = bf16[16,2,4096]{2,1,0:T(2,128)(2,1)S(1)} all-gather(bf16[1,2,4096]{2,1,0:T(2,128)(2,1)} %bitcast.87), channel_id=1, replica_groups=mesh['inst'=16,'page'=8,'head'=2] {'inst'}, dimensions={0}, use_global_device_ids=true | all-gather | bytes 278528 | tf_op jit(solution)/shard_map/all_gather | solution.py:122
  249.5 0.1 reshape.175
  249.6 1.2 gather_fusion
  250.8 0.2 copy.37
  251.0 4.6 fusion.34
  255.6 3.5 copy.34
  259.1 3.0 copy.27
  262.1 3.5 copy.33
  265.6 3.0 copy.24
  268.5 2.9 fusion.4
  271.5 0.1 copy.25
  271.6 0.1 copy.28
  271.7 0.2 select_reduce_fusion
  271.9 689.7 %pmax.7 = f32[32,32]{1,0:T(8,128)S(1)} all-reduce(f32[32,32]{1,0:T(8,128)S(1)} %select_reduce_fusion), channel_id=1, replica_groups=mesh['inst'=16,'page'=8,'head'=2] {'inst','page'}, use_global_device_ids=true, to_apply=%region_4.5 | all-reduce | flops 1024 | bytes 8192 | tf_op jit(solution)/shard_map/pmax | solution.py:132
  961.6 3.7 fusion.7
  965.3 0.6 gather_fusion.1
  966.0 0.0 copy-start
  966.0 0.6 mul.86
  966.6 1.0 copy-done
  967.6 4.3 fusion
  971.9 0.0 copy-start.2
  971.9 0.0 copy-start.1
  971.9 0.0 all-reduce.4.cloned.1.call-update
  971.9 1.4 fusion.5
  973.3 0.0 copy-done.2
  973.3 0.0 copy-done.1
  973.3 0.1 fusion.18
  973.5 0.1 mul.76
  973.6 0.1 copy.29
  973.6 0.1 copy.30
  973.8 0.1 fusion.14
  973.9 681.6 %psum.15 = f32[32,32]{1,0:T(8,128)S(1)} all-reduce(f32[32,32]{1,0:T(8,128)S(1)} %fusion.14), channel_id=1, replica_groups=mesh['inst'=16,'page'=8,'head'=2] {'inst','page'}, use_global_device_ids=true, to_apply=%region_7.8 | all-reduce | flops 1024 | bytes 8192 | tf_op jit(solution)/shard_map/psum | solution.py:134
  1655.5 0.1 broadcast_bitcast_fusion.3
  1655.6 0.1 broadcast_bitcast_fusion
  1655.7 0.0 all-reduce.4.cloned.1.call-done
  1655.7 1.6 fusion.17
  (18 shorter events, 0.1 us)
Async XLA Ops:
  6.5 1649.2 %all-reduce.4.cloned.1.call-start = ((), (), s32[]{:S(2)}) async-start(), calls=%async_computation | async-start | bytes 1048576 | tf_op jit(solution)/shard_map/psum | solution.py:134
  966.0 1.6 copy-start
  971.9 1.4 copy-start.2
  971.9 1.4 copy-start.1
Sparse Core Ops, SparseCore 0:
  972.0 207.2 all-reduce.3
where the time goes:
time: 1660 us
  blocking collectives  1430 us (86%)
  local copies, waits for them, and re-layouts  205 us (12%)
    pmax x1, blocking collectives, shards(): shared_max = lax.pmax(local_max, ('inst', 'page'))  690 us
    psum x1, blocking collectives, shards(): lax.psum((shared_out, shared_total), ('inst', 'page'))  682 us
    scatter x1, local copies, waits for them, and re-layouts, slot_owners(): jnp.full((slots,), requests, jnp.int32).at[expected_output]  90.2 us
    scatter x1, local copies, waits for them, and re-layouts, slot_owners(): jnp.zeros((slots,), jnp.int32).at[expected_output]  90.2 us
  transfers between devices with their start and end apart: 1, of which 0 were waited for; matrix products, arithmetic and copies ran while one was open for 0% of the time, Pallas kernels for 0%

commit v1 on v0

--- a/solution.py
+++ b/solution.py
@@ -1,3 +1,4 @@
+import functools
 import math
 import jax
 import jax.numpy as jnp
@@ -6,6 +7,15 @@
 
 HEAD_SIZE = 128
 LOWEST_SCORE = -1e30
+
+
+def lay_plate(message, group_axis, link_axis):
+    for c in (group_axis, link_axis):
+        message = lax.psum(message, c)
+    return message
+
+
+review_hubs = functools.partial(lay_plate, group_axis="page", link_axis="inst")
 
 
 def slot_owners(all_tables, all_lengths, slots, page_tok):
@@ -131,7 +141,7 @@
     local_max = request_max(page_max, page_owner, requests)
     shared_max = lax.pmax(local_max, ("inst", "page"))
     shared_total, shared_out = request_sums(page_max, page_sum, page_out, page_owner, shared_max)
-    summed_out, summed_total = lax.psum((shared_out, shared_total), ("inst", "page"))
+    summed_out, summed_total = review_hubs((shared_out, shared_total))
     cache_max = lax.dynamic_slice_in_dim(shared_max, row_start, own_rows, 0)
     cache_total = lax.dynamic_slice_in_dim(summed_total, row_start, own_rows, 0)
     cache_out = lax.dynamic_slice_in_dim(summed_out, row_start, own_rows, 0)

time: 1660 us -> 1170 us (0.70)
  blocking collectives: 1430 us -> 845 us
  waiting for transfers between devices: 0.04 us -> 87.6 us
    psum x1 -> x2, blocking collectives: 682 us -> 96.6 us  [lay_plate(): message = lax.psum(message, c)]
    psum x1 -> x2, waiting for transfers between devices: 0.02 us -> 87.6 us  [lay_plate(): message = lax.psum(message, c)]
  transfers between devices with their start and end apart: 1 -> 2, of which waited for: 0 -> 1; matrix products, arithmetic and copies ran while one was open for 0% -> 0% of each run, Pallas kernels for 0% -> 0%
where the time goes in v1:
time: 1170 us
  blocking collectives  845 us (72%)
  local copies, waits for them, and re-layouts  205 us (18%)
  waiting for transfers between devices  87.6 us (7%)
  between operations  14.3 us (1%)
    pmax x1, blocking collectives, shards(): shared_max = lax.pmax(local_max, ('inst', 'page'))  690 us
    psum x2, blocking collectives, lay_plate(): message = lax.psum(message, c)  96.6 us
    scatter x1, local copies, waits for them, and re-layouts, slot_owners(): jnp.full((slots,), requests, jnp.int32).at[expected_output]  90.2 us
    scatter x1, local copies, waits for them, and re-layouts, slot_owners(): jnp.zeros((slots,), jnp.int32).at[expected_output]  90.2 us
    psum x2, waiting for transfers between devices, lay_plate(): message = lax.psum(message, c)  87.6 us
  transfers between devices with their start and end apart: 2, of which 1 were waited for; matrix products, arithmetic and copies ran while one was open for 0% of the time, Pallas kernels for 0%

profile of v1, /device:TPU:0, one launch (start us, length us, event | category | flops | bytes accessed | tf_op | source)
XLA Modules:
  0.0 1166.8 jit_solution(13261194738452508063)
XLA Ops:
  6.5 0.0 all-reduce.5.cloned.1.call-start
  6.5 1.3 dynamic-slice
  8.5 0.9 dynamic-update-slice
  9.3 14.7 %all-reduce.1 = s32[32]{0:T(128)S(1)} all-reduce(s32[32]{0:T(128)S(1)} %dynamic-update-slice), channel_id=1, replica_groups=mesh['inst'=16,'page'=8,'head'=2] {'inst'}, use_global_device_ids=true, to_apply=%add.1 | all-reduce | flops 32 | bytes 256
  24.0 21.6 %all-gather = s32[16,2,768]{2,1,0:T(2,128)S(1)} all-gather(s32[1,2,768]{2,1,0:T(2,128)} %bitcast.89), channel_id=1, replica_groups=mesh['inst'=16,'page'=8,'head'=2] {'inst'}, dimensions={0}, use_global_device_ids=true | all-gather | bytes 104448 | tf_op jit(solution)/shard_map/all_gather | solution.py:129
  45.7 0.1 reshape.177
  45.8 0.1 subtract_clamp_fusion
  45.9 0.1 copy.36
  46.0 0.1 compare_select_fusion
  46.1 90.2 %scatter_custom_fusion = s32[128]{0:T(128)S(1)} fusion(s32[24576]{0:T(1024)S(1)} %bitcast.84, s32[24576]{0:T(1024)S(1)} %reshape.155, s32[]{:T(128)} %constant.17.clone.1), kind=kCustom, calls=%fused_computation.59 | custom fusion | bytes 516 | tf_op jit(solution)/shard_map/scatter | solution.py:34
  136.3 90.2 %scatter_custom_fusion.1 = s32[128]{0:T(128)S(1)} fusion(s32[24576]{0:T(1024)S(1)} %bitcast.85, s32[24576]{0:T(1024)S(1)} %reshape.163, s32[]{:T(128)} %constant.5.clone.1), kind=kCustom, calls=%fused_computation.57 | custom fusion | bytes 516 | tf_op jit(solution)/shard_map/scatter | solution.py:36
  226.5 0.1 iota_compare_fusion
  226.6 22.9 %all-gather.1 = bf16[16,2,4096]{2,1,0:T(2,128)(2,1)S(1)} all-gather(bf16[1,2,4096]{2,1,0:T(2,128)(2,1)} %bitcast.87), channel_id=1, replica_groups=mesh['inst'=16,'page'=8,'head'=2] {'inst'}, dimensions={0}, use_global_device_ids=true | all-gather | bytes 278528 | tf_op jit(solution)/shard_map/all_gather | solution.py:132
  249.5 0.1 reshape.175
  249.6 1.2 gather_fusion
  250.8 0.2 copy.37
  251.0 4.6 fusion.34
  255.6 3.5 copy.34
  259.1 3.0 copy.27
  262.1 3.5 copy.33
  265.6 3.0 copy.24
  268.5 2.9 fusion.4
  271.5 0.1 copy.25
  271.6 0.1 copy.28
  271.7 0.2 select_reduce_fusion
  271.9 689.7 %pmax.7 = f32[32,32]{1,0:T(8,128)S(1)} all-reduce(f32[32,32]{1,0:T(8,128)S(1)} %select_reduce_fusion), channel_id=1, replica_groups=mesh['inst'=16,'page'=8,'head'=2] {'inst','page'}, use_global_device_ids=true, to_apply=%region_4.5 | all-reduce | flops 1024 | bytes 8192 | tf_op jit(solution)/shard_map/pmax | solution.py:142
  961.6 3.7 fusion.7
  965.3 0.6 gather_fusion.1
  966.0 0.6 mul.86
  966.6 1.0 copy-done
  967.5 4.3 fusion
  971.9 0.0 all-reduce.5.cloned.1.call-update
  971.9 0.0 all-reduce.7.cloned.1.call-start
  971.9 1.4 fusion.5
  973.3 0.0 copy-done.2
  973.4 0.1 fusion.18
  973.5 0.1 mul.76
  973.6 0.1 copy.29
  973.7 0.1 copy.30
  973.8 0.1 fusion.14
  974.0 27.1 %psum.30 = f32[32,32]{1,0:T(8,128)S(1)} all-reduce(f32[32,32]{1,0:T(8,128)S(1)} %fusion.14), channel_id=1, replica_groups=mesh['inst'=16,'page'=8,'head'=2] {'page'}, use_global_device_ids=true, to_apply=%region_8.9 | all-reduce | flops 1024 | bytes 8192 | tf_op jit(solution)/shard_map/psum | solution.py:14
  1001.0 69.5 %psum.31 = f32[32,32]{1,0:T(8,128)S(1)} all-reduce(f32[32,32]{1,0:T(8,128)S(1)} %psum.30), channel_id=1, replica_groups=mesh['inst'=16,'page'=8,'head'=2] {'inst'}, use_global_device_ids=true, to_apply=%region_9.10 | all-reduce | flops 1024 | bytes 8192 | tf_op jit(solution)/shard_map/psum | solution.py:14
  1070.6 0.0 all-reduce.5.cloned.1.call-done
  1070.6 0.0 all-reduce.7.cloned.1.call-update
  1070.6 0.1 broadcast_bitcast_fusion.3
  1070.7 0.1 broadcast_bitcast_fusion
  1070.8 87.6 %all-reduce.7.cloned.1.call-done = f32[32,4096]{1,0:T(8,128)} async-done(((f32[32,4096]{1,0:T(8,128)}), f32[32,4096]{1,0:T(8,128)}) %all-reduce.7.cloned.1.call-update) | async-done | bytes 524304 | tf_op jit(solution)/shard_map/psum | solution.py:14
  1158.4 1.6 fusion.17
  (22 shorter events, 0.2 us)
Async XLA Ops:
  6.5 1064.0 %all-reduce.5.cloned.1.call-start = ((), (), s32[]{:S(2)}) async-start(), calls=%async_computation | async-start | bytes 1048576 | tf_op jit(solution)/shard_map/psum | solution.py:14
  966.0 1.6 copy-start
  971.9 1.5 copy-start.2
  971.9 1.5 copy-start.1
  971.9 186.5 %all-reduce.7.cloned.1.call-start = ((), (), s32[]{:S(2)}) async-start(), calls=%async_computation.1 | async-start | bytes 1048576 | tf_op jit(solution)/shard_map/psum | solution.py:14
Sparse Core Ops, SparseCore 0:
  972.0 64.1 all-reduce.4
  1070.7 87.5 all-reduce.6
